TPU v7x, 512 devices: a whole 4x4x16 slice. The times are simulated.
512 devices in a mesh: var: 32 (over z_lo, y, core), head: 16 (over z_hi, x).
Axes of the slice: x: 4, y: 4, z: 16 (z_hi: 4, z_lo: 4; z = z_hi * 4 + z_lo), core: 2. Of those that a mesh axis runs over, the one named last changes fastest.
Arguments:
- queries: bfloat16 [16384, 8192], P('var', 'head'), may hold values from -5 to 5
- ablated: int32 [16384], P('var'), may hold values from 0 to 63
- head_keep: int32 [32, 64], P(None, 'head'), may hold values 0 or 1
- k_cache: bfloat16 [32, 2048, 1024], P('var', 'head'), may hold values from -4 to 4
- v_cache: bfloat16 [32, 2048, 1024], P('var', 'head'), may hold values from -40 to 40
- lengths: int32 [32], P('var'), may hold values from 512 to 2048, as said below
- out_weight: bfloat16 [8192, 4096], P('head', 'var'), may hold values from -0.125 to 0.125
- residual: bfloat16 [16384, 4096], P('var', 'head'), may hold values from -6 to 6
Outputs:
- patched: bfloat16 [16384, 4096], P('var', 'head')
Inputs may be any that keep to these rules, and one draw needn't show every extreme that they name: `lengths`: one prompt has exactly 2048 live positions.
All inputs are finite; a program needn't handle non-finite values. No bound on the sum of `head_keep` on one device may be relied on, other than what follows from the above.
Results may differ from a plain program's by a relative error of at most 0.012.
Values may be sent and summed in bfloat16 or wider, within the bound.
No kernel may reach another device: no remote copies, remote signals or barrier semaphores. Data moves between devices by JAX's collectives and lax.ppermute only.
A program may use at most 64 MiB of HBM per device.

v0:
```python
import math
import jax
import jax.numpy as jnp
from jax import lax
from jax.sharding import PartitionSpec as P

HEADS = 64
KVH = 8
HD = 128


def attend(query_rows, full_keys, full_values, prompt_length):
    local_heads = query_rows.shape[1]
    group_size = HEADS // KVH
    score_scale = 1.0 / math.sqrt(HD)
    visible = jnp.arange(full_keys.shape[0]) < prompt_length
    pieces_out = []
    for column_pair in range(local_heads // 2):
        kv_index = 2 * column_pair // group_size
        query_pair = query_rows[:, 2 * column_pair : 2 * column_pair + 2, :]
        scores = (
            jnp.einsum(
                "rhd,td->hrt",
                query_pair,
                full_keys[:, kv_index, :],
                preferred_element_type=jnp.float32,
            )
            * score_scale
        )
        scores = jnp.where(visible, scores, -jnp.inf)
        row_max = jnp.max(scores, axis=-1, keepdims=True)
        exponent = jnp.exp(scores - row_max)
        probs = (exponent / jnp.sum(exponent, axis=-1, keepdims=True)).astype(jnp.bfloat16)
        outputs = jnp.einsum(
            "hrt,td->rhd", probs, full_values[:, kv_index, :], preferred_element_type=jnp.float32
        )
        pieces_out.append(outputs.astype(jnp.bfloat16))
    return jnp.concatenate(pieces_out, axis=1)


def project(gated, out_weight):
    partial_value = jnp.dot(
        gated,
        lax.all_gather(out_weight, "var", axis=1, tiled=True),
        preferred_element_type=jnp.float32,
    )
    return lax.psum_scatter(
        partial_value.astype(jnp.bfloat16), "head", scatter_dimension=1, tiled=True
    )


def per_device(queries, ablated, head_keep, k_cache, v_cache, lengths, out_weight, residual):
    row_count, feature_count = queries.shape
    var_count = lax.axis_size("var")
    head_count = lax.axis_size("head")
    local_heads = head_keep.shape[1]
    per_prompt = row_count // var_count
    head_position = lax.axis_index("head")
    copies = max(1, head_count // KVH)
    local_positions = k_cache.shape[1]
    stacked = jnp.stack([k_cache[0], v_cache[0]]).reshape(2, local_positions, KVH, HD)
    stacked = jnp.repeat(stacked, copies, axis=2)
    arrived_kv = lax.all_to_all(stacked, "head", split_axis=2, concat_axis=1, tiled=True)
    full_keys = arrived_kv[0]
    full_values = arrived_kv[1]
    prompt_keep = jnp.repeat(head_keep, per_prompt, axis=0)
    heads_here = head_position * local_heads + jnp.arange(local_heads)
    kept_heads = jnp.where(ablated[:, None] != heads_here[None, :], prompt_keep, 0).astype(
        jnp.bfloat16
    )
    grouped = queries.reshape(var_count, per_prompt, feature_count)
    arrived = lax.all_to_all(grouped, "var", split_axis=0, concat_axis=0, tiled=True)
    head_out = attend(
        arrived.reshape(row_count, local_heads, HD), full_keys, full_values, lengths[0]
    )
    returned = lax.all_to_all(
        head_out.reshape(var_count, per_prompt, feature_count),
        "var",
        split_axis=0,
        concat_axis=0,
        tiled=True,
    )
    gated = (returned.reshape(row_count, local_heads, HD) * kept_heads[:, :, None]).reshape(
        row_count, feature_count
    )
    projected = project(gated, out_weight)
    return (residual.astype(jnp.float32) + projected.astype(jnp.float32)).astype(jnp.bfloat16)


def solution(mesh):
    return jax.shard_map(
        per_device,
        mesh=mesh,
        in_specs=(
            P("var", "head"),
            P("var"),
            P(None, "head"),
            P("var", "head", None),
            P("var", "head", None),
            P("var"),
            P("head", "var"),
            P("var", "head"),
        ),
        out_specs=P("var", "head"),
        check_vma=False,
    )
```

profile of v0, /device:TPU:8, one launch (start us, length us, event | category | flops | bytes accessed | tf_op | source)
XLA Modules:
  0.0 328.7 jit_solution(7150349831020283195)
XLA Ops:
  6.5 9.3 %all-to-all-start.1 = ((bf16[32,16,512]{2,1,0:T(8,128)(2,1)}), bf16[32,16,512]{2,1,0:T(8,128)(2,1)S(1)}, u32[]{:S(2)}, u32[]{:S(2)}) async-start(bf16[32,16,512]{2,1,0:T(8,128)(2,1)} %bitcast.62), calls=%async_computation.1 | async-start | bytes 1048576 | tf_op jit(solution)/shard_map/all_to_all | solution.py:72
  15.9 1.2 copy_bitcast_fusion
  17.0 13.6 %all-to-all-done.1 = bf16[32,16,512]{2,1,0:T(8,128)(2,1)S(1)} async-done(((bf16[32,16,512]{2,1,0:T(8,128)(2,1)}), bf16[32,16,512]{2,1,0:T(8,128)(2,1)S(1)}, u32[]{:S(2)}, u32[]{:S(2)}) %all-to-all-start.1) | async-done | bytes 524320 | tf_op jit(solution)/shard_map/all_to_all | solution.py:72
  30.7 1.2 broadcast_in_dim.27
  31.9 14.6 %all-to-all-start = ((bf16[2,128,16,128]{3,1,0,2:T(8,128)(2,1)}), bf16[2,128,16,128]{3,1,0,2:T(8,128)(2,1)S(1)}, u32[]{:S(2)}, u32[]{:S(2)}) async-start(bf16[2,128,16,128]{3,1,0,2:T(8,128)(2,1)} %bitcast), calls=%async_computation | async-start | bytes 2097152 | tf_op jit(solution)/shard_map/all_to_all | solution.py:63
  46.5 0.0 all-gather.2.cloned.1.call-start
  46.6 0.7 all-gather.2.cloned.1.call-update
  47.9 0.1 reshape.73
  48.0 0.4 fusion.46
  48.4 50.3 %all-to-all-done = bf16[2,128,16,128]{3,1,0,2:T(8,128)(2,1)S(1)} async-done(((bf16[2,128,16,128]{3,1,0,2:T(8,128)(2,1)}), bf16[2,128,16,128]{3,1,0,2:T(8,128)(2,1)S(1)}, u32[]{:S(2)}, u32[]{:S(2)}) %all-to-all-start) | async-done | bytes 1048608 | tf_op jit(solution)/shard_map/all_to_all | solution.py:63
  98.8 0.1 fusion.45
  98.9 6.1 %fusion.52 = (f32[2,512]{1,0:T(2,128)S(1)}, f32[2,512,2048]{1,2,0:T(8,128)}) fusion(pred[2048]{0:T(1024)(128)(4,1)S(1)} %iota_compare_fusion, bf16[2048,128,1]{1,0,2:T(8,128)(2,1)S(1)} %bitcast.66, bf16[512,2,128]{2,1,0:T(2,128)(2,1)S(1)} %get-tuple-element.7), kind=kOutput, calls=%fused_computation.51 | convolution fusion | flops 545261568 | bytes 9181184 | tf_op jit(solution)/shard_map/sub | solution.py:32
  104.9 6.1 %fusion.47 = (f32[2,512]{1,0:T(2,128)S(1)}, f32[2,512,2048]{1,2,0:T(8,128)}) fusion(pred[2048]{0:T(1024)(128)(4,1)S(1)} %iota_compare_fusion, bf16[2048,128,1]{1,0,2:T(8,128)(2,1)S(1)} %bitcast.67, bf16[512,2,128]{2,1,0:T(2,128)(2,1)S(1)} %get-tuple-element.8), kind=kOutput, calls=%fused_computation.50 | convolution fusion | flops 545261568 | bytes 9181184 | tf_op jit(solution)/shard_map/sub | solution.py:32
  111.0 0.0 copy-start.3
  111.0 4.3 %fusion.20 = bf16[512,2,128]{0,2,1:T(8,128)(2,1)S(1)} fusion(bf16[2048,128,1]{1,0,2:T(8,128)(2,1)S(1)} %bitcast.64, f32[2,512,2048]{1,2,0:T(8,128)} %get-tuple-element.12, f32[2,512]{1,0:T(2,128)S(1)} %get-tuple-element.11), kind=kOutput, calls=%fused_computation.25 | convolution fusion | flops 541196288 | bytes 9179136 | tf_op jit(solution)/shard_map/hrt,td->rhd/dot_general | solution.py:34
  115.3 1.5 copy-done.3
  116.8 0.0 copy-start.1
  116.8 0.0 copy-start.2
  116.8 0.8 fusion.21
  117.7 0.3 copy.27
  118.0 1.0 reshape.74
  119.0 11.7 %all-to-all-start.2 = ((bf16[32,16,512]{2,1,0:T(8,128)(2,1)}), bf16[32,16,512]{2,1,0:T(8,128)(2,1)S(1)}, u32[]{:S(2)}, u32[]{:S(2)}) async-start(bf16[32,16,512]{2,1,0:T(8,128)(2,1)} %reshape.74), calls=%async_computation.2 | async-start | bytes 1048576 | tf_op jit(solution)/shard_map/all_to_all | solution.py:76
  130.6 0.2 reduce-scatter.2.cloned.1.call-start
  130.9 0.0 copy-done.1
  130.9 0.1 broadcast_in_dim.30
  131.0 0.1 reshape.76
  131.1 0.0 copy-done.2
  131.1 0.1 select_convert_fusion
  131.2 0.2 copy.28
  131.3 0.0 copy-start
  131.4 15.4 %all-to-all-done.2 = bf16[32,16,512]{2,1,0:T(8,128)(2,1)S(1)} async-done(((bf16[32,16,512]{2,1,0:T(8,128)(2,1)}), bf16[32,16,512]{2,1,0:T(8,128)(2,1)S(1)}, u32[]{:S(2)}, u32[]{:S(2)}) %all-to-all-start.2) | async-done | bytes 524320 | tf_op jit(solution)/shard_map/all_to_all | solution.py:76
  146.7 2.9 all-gather.2.cloned.1.call-done
  149.6 0.6 mul.25
  150.2 6.5 %convolution_convert_fusion = bf16[512,4096]{1,0:T(8,128)(2,1)} fusion(bf16[512,4096]{1,0:T(8,128)(2,1)} %all-gather.2.cloned.1.call-done, bf16[512,512]{1,0:T(8,128)(2,1)S(1)} %bitcast.63, bf16[64,8,4,128]{3,2,1,0:T(4,128)(2,1)S(1)} %bitcast.61), kind=kOutput, calls=%fused_computation.14 | convolution fusion | flops 2149842944 | bytes 9437184 | tf_op jit(solution)/shard_map/dot_general | solution.py:42
  156.7 0.0 reduce-scatter.2.cloned.1.call-update
  156.7 163.5 %reduce-scatter.2.cloned.1.call-done = bf16[512,256]{1,0:T(8,128)(2,1)} async-done(((bf16[512,4096]{1,0:T(8,128)(2,1)}), bf16[512,256]{1,0:T(8,128)(2,1)}) %reduce-scatter.2.cloned.1.call-update) | async-done | bytes 262160 | tf_op jit(solution)/shard_map/reduce_scatter | solution.py:47
  320.1 0.0 copy-done
  320.1 1.7 add_convert_fusion
  (3 shorter events, 0.1 us)
Async XLA Ops:
  6.5 24.1 %all-to-all-start.1 = ((bf16[32,16,512]{2,1,0:T(8,128)(2,1)}), bf16[32,16,512]{2,1,0:T(8,128)(2,1)S(1)}, u32[]{:S(2)}, u32[]{:S(2)}) async-start(bf16[32,16,512]{2,1,0:T(8,128)(2,1)} %bitcast.62), calls=%async_computation.1 | async-start | bytes 1048576 | tf_op jit(solution)/shard_map/all_to_all | solution.py:72
  31.9 66.9 %all-to-all-start = ((bf16[2,128,16,128]{3,1,0,2:T(8,128)(2,1)}), bf16[2,128,16,128]{3,1,0,2:T(8,128)(2,1)S(1)}, u32[]{:S(2)}, u32[]{:S(2)}) async-start(bf16[2,128,16,128]{3,1,0,2:T(8,128)(2,1)} %bitcast), calls=%async_computation | async-start | bytes 2097152 | tf_op jit(solution)/shard_map/all_to_all | solution.py:63
  46.5 103.0 %all-gather.2.cloned.1.call-start = ((), (), s32[]{:S(2)}) async-start(), calls=%async_computation.4 | async-start | bytes 4325376 | tf_op jit(solution)/shard_map/all_gather | solution.py:44
  111.0 5.8 %copy-start.3 = (f32[2,512,2048]{1,2,0:T(8,128)S(1)}, f32[2,512,2048]{1,2,0:T(8,128)}, u32[]{:S(2)}) copy-start(f32[2,512,2048]{1,2,0:T(8,128)} %get-tuple-element.10) | copy-start | bytes 25165828
  116.8 14.1 %copy-start.1 = (s32[32,4]{0,1:T(4,128)S(1)}, s32[32,4]{0,1:T(4,128)}, u32[]{:S(2)}) copy-start(s32[32,4]{0,1:T(4,128)} %param.10) | copy-start | bytes 1540
  116.8 14.3 %copy-start.2 = (s32[512]{0:T(512)S(1)}, s32[512]{0:T(512)}, u32[]{:S(2)}) copy-start(s32[512]{0:T(512)} %param.9) | copy-start | bytes 6148
  119.0 27.8 %all-to-all-start.2 = ((bf16[32,16,512]{2,1,0:T(8,128)(2,1)}), bf16[32,16,512]{2,1,0:T(8,128)(2,1)S(1)}, u32[]{:S(2)}, u32[]{:S(2)}) async-start(bf16[32,16,512]{2,1,0:T(8,128)(2,1)} %reshape.74), calls=%async_computation.2 | async-start | bytes 1048576 | tf_op jit(solution)/shard_map/all_to_all | solution.py:76
  130.6 189.5 %reduce-scatter.2.cloned.1.call-start = ((), (), s32[]{:S(2)}) async-start(), calls=%async_computation.5 | async-start | bytes 4456448 | tf_op jit(solution)/shard_map/reduce_scatter | solution.py:47
  131.3 188.8 %copy-start = (bf16[512,256]{1,0:T(8,128)(2,1)S(1)}, bf16[512,256]{1,0:T(8,128)(2,1)}, u32[]{:S(2)}) copy-start(bf16[512,256]{1,0:T(8,128)(2,1)} %param.15) | copy-start | bytes 786436
Sparse Core Ops, SparseCore 0:
  49.4 100.1 all-gather.1
  156.8 163.2 reduce-scatter.1
where the time goes:
time: 329 us
  waiting for transfers between devices  246 us (75%)
  starting transfers between devices  35.9 us (11%)
  matrix products  23.6 us (7%)
  between operations  14.2 us (4%)
  local copies, waits for them, and re-layouts  5.61 us (2%)
    reduce_scatter x1, waiting for transfers between devices, project(): lax.psum_scatter(partial_value.astype(jnp.bfloat16), 'head', scatter_dime...  163 us
    all_to_all x1, waiting for transfers between devices, per_device(): lax.all_to_all(stacked, 'head', split_axis=2, concat_axis=1, tiled=True)  50.3 us
    all_to_all x1, waiting for transfers between devices, per_device(): lax.all_to_all(head_out.reshape(var_count, per_prompt, feature_count), 'v...  15.4 us
    all_to_all x1, starting transfers between devices, per_device(): lax.all_to_all(stacked, 'head', split_axis=2, concat_axis=1, tiled=True)  14.6 us
    all_to_all x1, waiting for transfers between devices, per_device(): lax.all_to_all(grouped, 'var', split_axis=0, concat_axis=0, tiled=True)  13.6 us
    sub x2, matrix products, attend(): exponent = jnp.exp(scores - row_max)  12.2 us
    all_to_all x1, starting transfers between devices, per_device(): lax.all_to_all(head_out.reshape(var_count, per_prompt, feature_count), 'v...  11.7 us
    all_to_all x1, starting transfers between devices, per_device(): lax.all_to_all(grouped, 'var', split_axis=0, concat_axis=0, tiled=True)  9.34 us
  transfers between devices with their start and end apart: 5, of which 5 were waited for; matrix products, arithmetic and copies ran while one was open for 6% of the time, Pallas kernels for 0%

commit v1 on v0

--- a/solution.py
+++ b/solution.py
@@ -60,7 +60,15 @@
     local_positions = k_cache.shape[1]
     stacked = jnp.stack([k_cache[0], v_cache[0]]).reshape(2, local_positions, KVH, HD)
     stacked = jnp.repeat(stacked, copies, axis=2)
-    arrived_kv = lax.all_to_all(stacked, "head", split_axis=2, concat_axis=1, tiled=True)
+    arrived_kv = jnp.concatenate(
+        jax.lax.all_to_all(
+            jnp.stack(jnp.split(stacked, jax.lax.psum(1, axis_name="head"), 2), 0),
+            split_axis=0,
+            concat_axis=0,
+            axis_name="head",
+        ),
+        1,
+    )
     full_keys = arrived_kv[0]
     full_values = arrived_kv[1]
     prompt_keep = jnp.repeat(head_keep, per_prompt, axis=0)

time: 329 us -> 326 us (level)
  waiting for transfers between devices: 246 us -> 234 us
  local copies, waits for them, and re-layouts: 5.61 us -> 14.7 us
    all_to_all x1, waiting for transfers between devices: 13.6 us -> 3.3 us  [per_device(): lax.all_to_all(grouped, 'var', split_axis=0, concat_axis=0, tiled=True)]
    unnamed x8 -> x23, local copies, waits for them, and re-layouts: 1.55 us -> 10.9 us
  transfers between devices with their start and end apart: 5 -> 5, of which waited for: 5 -> 5; matrix products, arithmetic and copies ran while one was open for 6% -> 10% of each run, Pallas kernels for 0% -> 0%
where the time goes in v1:
time: 326 us
  waiting for transfers between devices  234 us (72%)
  starting transfers between devices  35.9 us (11%)
  matrix products  23.6 us (7%)
  local copies, waits for them, and re-layouts  14.7 us (5%)
  between operations  14.2 us (4%)
    reduce_scatter x1, waiting for transfers between devices, project(): lax.psum_scatter(partial_value.astype(jnp.bfloat16), 'head', scatter_dime...  162 us
    all_to_all x1, waiting for transfers between devices, per_device(): jax.lax.all_to_all(jnp.stack(jnp.split(stacked, jax.lax.psum(1, axis_name...  50.3 us
    all_to_all x1, waiting for transfers between devices, per_device(): lax.all_to_all(head_out.reshape(var_count, per_prompt, feature_count), 'v...  15.4 us
    all_to_all x1, starting transfers between devices, per_device(): jax.lax.all_to_all(jnp.stack(jnp.split(stacked, jax.lax.psum(1, axis_name...  14.6 us
    sub x2, matrix products, attend(): exponent = jnp.exp(scores - row_max)  12.2 us
    all_to_all x1, starting transfers between devices, per_device(): lax.all_to_all(head_out.reshape(var_count, per_prompt, feature_count), 'v...  11.7 us
    unnamed x23, local copies, waits for them, and re-layouts  10.9 us
    all_to_all x1, starting transfers between devices, per_device(): lax.all_to_all(grouped, 'var', split_axis=0, concat_axis=0, tiled=True)  9.34 us
  transfers between devices with their start and end apart: 5, of which 5 were waited for; matrix products, arithmetic and copies ran while one was open for 10% of the time, Pallas kernels for 0%

profile of v1, /device:TPU:8, one launch (start us, length us, event | category | flops | bytes accessed | tf_op | source)
XLA Modules:
  0.0 325.7 jit_solution(12128147125843039491)
XLA Ops:
  6.5 9.3 %all-to-all-start.1 = ((bf16[32,16,512]{2,1,0:T(8,128)(2,1)}), bf16[32,16,512]{2,1,0:T(8,128)(2,1)S(1)}, u32[]{:S(2)}, u32[]{:S(2)}) async-start(bf16[32,16,512]{2,1,0:T(8,128)(2,1)} %bitcast.170), calls=%async_computation.1 | async-start | bytes 1048576 | tf_op jit(solution)/shard_map/all_to_all | solution.py:80
  15.9 1.2 copy_bitcast_fusion
  17.0 0.3 broadcast_in_dim.27
  17.3 0.6 fusion.56
  18.0 0.6 fusion.55
  18.6 0.6 fusion.54
  19.2 0.6 fusion.53
  19.9 0.6 fusion.52
  20.5 0.6 fusion.51
  21.1 0.6 fusion.50
  21.7 0.6 fusion.49
  22.4 0.6 fusion.48
  23.0 0.6 fusion.47
  23.6 0.6 fusion.46
  24.2 0.6 fusion.45
  24.8 0.6 fusion.44
  25.5 0.6 fusion.43
  26.1 0.6 fusion.42
  26.7 0.6 fusion.41
  27.4 3.3 %all-to-all-done.1 = bf16[32,16,512]{2,1,0:T(8,128)(2,1)S(1)} async-done(((bf16[32,16,512]{2,1,0:T(8,128)(2,1)}), bf16[32,16,512]{2,1,0:T(8,128)(2,1)S(1)}, u32[]{:S(2)}, u32[]{:S(2)}) %all-to-all-start.1) | async-done | bytes 524320 | tf_op jit(solution)/shard_map/all_to_all | solution.py:80
  30.7 14.6 %all-to-all-start = ((bf16[16,2,128,1,128]{4,2,3,1,0:T(8,128)(2,1)}), bf16[16,2,128,1,128]{4,2,3,1,0:T(8,128)(2,1)S(1)}, u32[]{:S(2)}, u32[]{:S(2)}) async-start(bf16[16,2,128,1,128]{4,2,3,1,0:T(8,128)(2,1)} %fusion.41), calls=%async_computation | async-start | bytes 2097152 | tf_op jit(solution)/shard_map/all_to_all | solution.py:64
  45.3 0.0 all-gather.2.cloned.1.call-start
  45.4 0.7 all-gather.2.cloned.1.call-update
  46.7 0.1 reshape.78
  46.8 0.4 fusion.62
  47.2 50.3 %all-to-all-done = bf16[16,2,128,1,128]{4,2,3,1,0:T(8,128)(2,1)S(1)} async-done(((bf16[16,2,128,1,128]{4,2,3,1,0:T(8,128)(2,1)}), bf16[16,2,128,1,128]{4,2,3,1,0:T(8,128)(2,1)S(1)}, u32[]{:S(2)}, u32[]{:S(2)}) %all-to-all-start) | async-done | bytes 1048608 | tf_op jit(solution)/shard_map/all_to_all | solution.py:64
  97.5 0.1 fusion.61
  97.6 6.1 %fusion.68 = (f32[2,512]{1,0:T(2,128)S(1)}, f32[2,512,2048]{1,2,0:T(8,128)}) fusion(pred[2048]{0:T(1024)(128)(4,1)S(1)} %iota_compare_fusion, bf16[2048,128,1]{1,0,2:T(8,128)(2,1)S(1)} %bitcast.174, bf16[512,2,128]{2,1,0:T(2,128)(2,1)S(1)} %get-tuple-element.7), kind=kOutput, calls=%fused_computation.83 | convolution fusion | flops 545261568 | bytes 9181184 | tf_op jit(solution)/shard_map/sub | solution.py:32
  103.7 6.1 %fusion.63 = (f32[2,512]{1,0:T(2,128)S(1)}, f32[2,512,2048]{1,2,0:T(8,128)}) fusion(pred[2048]{0:T(1024)(128)(4,1)S(1)} %iota_compare_fusion, bf16[2048,128,1]{1,0,2:T(8,128)(2,1)S(1)} %bitcast.175, bf16[512,2,128]{2,1,0:T(2,128)(2,1)S(1)} %get-tuple-element.8), kind=kOutput, calls=%fused_computation.82 | convolution fusion | flops 545261568 | bytes 9181184 | tf_op jit(solution)/shard_map/sub | solution.py:32
  109.8 4.3 %fusion.20 = bf16[512,2,128]{0,2,1:T(8,128)(2,1)S(1)} fusion(bf16[2048,128,1]{1,0,2:T(8,128)(2,1)S(1)} %bitcast.172, f32[2,512,2048]{1,2,0:T(8,128)} %get-tuple-element.12, f32[2,512]{1,0:T(2,128)S(1)} %get-tuple-element.11), kind=kOutput, calls=%fused_computation.25 | convolution fusion | flops 541196288 | bytes 9179136 | tf_op jit(solution)/shard_map/hrt,td->rhd/dot_general | solution.py:34
  114.1 1.5 copy-done.3
  115.6 0.8 fusion.21
  116.4 0.3 copy.72
  116.8 1.0 reshape.79
  117.7 11.7 %all-to-all-start.2 = ((bf16[32,16,512]{2,1,0:T(8,128)(2,1)}), bf16[32,16,512]{2,1,0:T(8,128)(2,1)S(1)}, u32[]{:S(2)}, u32[]{:S(2)}) async-start(bf16[32,16,512]{2,1,0:T(8,128)(2,1)} %reshape.79), calls=%async_computation.2 | async-start | bytes 1048576 | tf_op jit(solution)/shard_map/all_to_all | solution.py:84
  129.4 0.2 reduce-scatter.2.cloned.1.call-start
  129.7 0.1 broadcast_in_dim.30
  129.7 0.1 reshape.81
  129.9 0.1 select_convert_fusion
  129.9 0.2 copy.73
  130.1 0.0 copy-start
  130.1 15.4 %all-to-all-done.2 = bf16[32,16,512]{2,1,0:T(8,128)(2,1)S(1)} async-done(((bf16[32,16,512]{2,1,0:T(8,128)(2,1)}), bf16[32,16,512]{2,1,0:T(8,128)(2,1)S(1)}, u32[]{:S(2)}, u32[]{:S(2)}) %all-to-all-start.2) | async-done | bytes 524320 | tf_op jit(solution)/shard_map/all_to_all | solution.py:84
  145.5 2.8 all-gather.2.cloned.1.call-done
  148.3 0.6 mul.25
  149.0 6.5 %convolution_convert_fusion = bf16[512,4096]{1,0:T(8,128)(2,1)} fusion(bf16[512,4096]{1,0:T(8,128)(2,1)} %all-gather.2.cloned.1.call-done, bf16[512,512]{1,0:T(8,128)(2,1)S(1)} %bitcast.171, bf16[64,8,4,128]{3,2,1,0:T(4,128)(2,1)S(1)} %bitcast.169), kind=kOutput, calls=%fused_computation.14 | convolution fusion | flops 2149842944 | bytes 9437184 | tf_op jit(solution)/shard_map/dot_general | solution.py:42
  155.4 0.0 reduce-scatter.2.cloned.1.call-update
  155.5 161.7 %reduce-scatter.2.cloned.1.call-done = bf16[512,256]{1,0:T(8,128)(2,1)} async-done(((bf16[512,4096]{1,0:T(8,128)(2,1)}), bf16[512,256]{1,0:T(8,128)(2,1)}) %reduce-scatter.2.cloned.1.call-update) | async-done | bytes 262160 | tf_op jit(solution)/shard_map/reduce_scatter | solution.py:47
  317.2 1.7 add_convert_fusion
  (9 shorter events, 0.1 us)
Async XLA Ops:
  6.5 24.1 %all-to-all-start.1 = ((bf16[32,16,512]{2,1,0:T(8,128)(2,1)}), bf16[32,16,512]{2,1,0:T(8,128)(2,1)S(1)}, u32[]{:S(2)}, u32[]{:S(2)}) async-start(bf16[32,16,512]{2,1,0:T(8,128)(2,1)} %bitcast.170), calls=%async_computation.1 | async-start | bytes 1048576 | tf_op jit(solution)/shard_map/all_to_all | solution.py:80
  30.7 66.9 %all-to-all-start = ((bf16[16,2,128,1,128]{4,2,3,1,0:T(8,128)(2,1)}), bf16[16,2,128,1,128]{4,2,3,1,0:T(8,128)(2,1)S(1)}, u32[]{:S(2)}, u32[]{:S(2)}) async-start(bf16[16,2,128,1,128]{4,2,3,1,0:T(8,128)(2,1)} %fusion.41), calls=%async_computation | async-start | bytes 2097152 | tf_op jit(solution)/shard_map/all_to_all | solution.py:64
  45.3 103.0 %all-gather.2.cloned.1.call-start = ((), (), s32[]{:S(2)}) async-start(), calls=%async_computation.4 | async-start | bytes 4325376 | tf_op jit(solution)/shard_map/all_gather | solution.py:44
  109.8 5.8 %copy-start.3 = (f32[2,512,2048]{1,2,0:T(8,128)S(1)}, f32[2,512,2048]{1,2,0:T(8,128)}, u32[]{:S(2)}) copy-start(f32[2,512,2048]{1,2,0:T(8,128)} %get-tuple-element.10) | copy-start | bytes 25165828
  115.6 14.1 %copy-start.1 = (s32[32,4]{0,1:T(4,128)S(1)}, s32[32,4]{0,1:T(4,128)}, u32[]{:S(2)}) copy-start(s32[32,4]{0,1:T(4,128)} %param.10) | copy-start | bytes 1540
  115.6 14.3 %copy-start.2 = (s32[512]{0:T(512)S(1)}, s32[512]{0:T(512)}, u32[]{:S(2)}) copy-start(s32[512]{0:T(512)} %param.9) | copy-start | bytes 6148
  117.7 27.8 %all-to-all-start.2 = ((bf16[32,16,512]{2,1,0:T(8,128)(2,1)}), bf16[32,16,512]{2,1,0:T(8,128)(2,1)S(1)}, u32[]{:S(2)}, u32[]{:S(2)}) async-start(bf16[32,16,512]{2,1,0:T(8,128)(2,1)} %reshape.79), calls=%async_computation.2 | async-start | bytes 1048576 | tf_op jit(solution)/shard_map/all_to_all | solution.py:84
  129.4 187.8 %reduce-scatter.2.cloned.1.call-start = ((), (), s32[]{:S(2)}) async-start(), calls=%async_computation.5 | async-start | bytes 4456448 | tf_op jit(solution)/shard_map/reduce_scatter | solution.py:47
  130.1 187.1 %copy-start = (bf16[512,256]{1,0:T(8,128)(2,1)S(1)}, bf16[512,256]{1,0:T(8,128)(2,1)}, u32[]{:S(2)}) copy-start(bf16[512,256]{1,0:T(8,128)(2,1)} %param.15) | copy-start | bytes 786436
Sparse Core Ops, SparseCore 0:
  48.2 100.1 all-gather.1
  155.6 161.5 reduce-scatter.1
